TPU v7x, 256 devices: a whole 4x4x8 slice. The times are simulated.
256 devices in a mesh: expert: 128 (over z, y, x), dp: 2 (over core).
Axes of the slice: x: 4, y: 4, z: 8, core: 2. Of those that a mesh axis runs over, the one named last changes fastest.
Arguments:
- layer_input: bfloat16 [32768, 3584], P(('expert', 'dp')), may hold values from -6 to 6
- out_grad: bfloat16 [32768, 3584], P(('expert', 'dp')), may hold values from -6 to 6
- routes: int32 [32768, 8], P(('expert', 'dp')), may hold values from 0 to 255, as said below
- gate_values: float32 [32768, 8], P(('expert', 'dp')), may hold values from 0.1 to 1
- keep_mask: int32 [32768, 8], P(('expert', 'dp')), may hold values 0 or 1
- gate_weight: bfloat16 [3584, 49152], P('dp', 'expert'), may hold values from -0.09375 to 0.09375
- up_weight: bfloat16 [3584, 49152], P('dp', 'expert'), may hold values from -0.09375 to 0.09375
- down_transposed: bfloat16 [3584, 49152], P('dp', 'expert'), may hold values from -0.15625 to 0.15625
Outputs:
- input_grad: bfloat16 [32768, 3584], P(('expert', 'dp'))
- gate_grad: bfloat16 [3584, 49152], P('dp', 'expert')
- up_grad: bfloat16 [3584, 49152], P('dp', 'expert')
- down_grad: bfloat16 [3584, 49152], P('dp', 'expert')
Inputs may be any that keep to these rules, and one draw needn't show every extreme that they name: `routes`: each token names 8 different experts. Among one device's 128 tokens no expert is named more than 5 times; on every device some expert below 32 is named exactly 5 times, and one expert below 32 is named 5 times on every device.
All inputs are finite; a program needn't handle non-finite values. No bound on the sum of `keep_mask` on one device may be relied on, other than what follows from the above.
Results may differ from a plain program's by a relative error of at most 0.0065.
Values may be sent and summed in bfloat16 or wider, within the bound.
A program may use at most 128 MiB of HBM per device.

v0:
```python
import jax
import jax.numpy as jnp
from jax import lax
from jax.sharding import PartitionSpec as P

TOP = 8
SPLIT = 4
MOST = 5


def as_sent(array):
    return jax.tree.map(lambda a: a.astype(jnp.bfloat16) if a.dtype == jnp.float32 else a, array)


def silu_parts(pre_gate):
    sigma = jax.nn.sigmoid(pre_gate)
    return (pre_gate * sigma, sigma * (1.0 + pre_gate * (1.0 - sigma)))


def route_tables(routes, keep_mask, live_count, slot_count):
    flat_routes = routes.reshape(-1)
    flat_keep = keep_mask.reshape(-1)
    expert_iota = jnp.arange(live_count, dtype=jnp.int32)
    chosen = ((flat_routes[:, None] == expert_iota[None, :]) & (flat_keep[:, None] == 1)).astype(
        jnp.int32
    )
    route_ranks = jnp.cumsum(chosen, axis=0) - 1
    slot_iota = jnp.arange(slot_count, dtype=jnp.int32)
    matched = chosen[:, :, None] * (route_ranks[:, :, None] == slot_iota[None, None, :]).astype(
        jnp.int32
    )
    route_iota = jnp.arange(flat_routes.shape[0], dtype=jnp.int32)
    picked = jnp.sum(matched * route_iota[:, None, None], axis=0)
    filled = jnp.sum(matched, axis=0)
    return (picked.reshape(-1), filled.reshape(-1))


def expert_backward(slot_inputs, slot_grads, weights):
    gate_full, up_full, down_full = weights
    pre_gate = jnp.dot(slot_inputs, gate_full, preferred_element_type=jnp.float32)
    pre_up = jnp.dot(slot_inputs, up_full, preferred_element_type=jnp.float32)
    activated, slope = silu_parts(pre_gate)
    hidden = (activated * pre_up).astype(jnp.bfloat16)
    hidden_grad = jnp.dot(slot_grads, down_full, preferred_element_type=jnp.float32)
    gate_side = (hidden_grad * pre_up * slope).astype(jnp.bfloat16)
    up_side = (hidden_grad * activated).astype(jnp.bfloat16)
    across = (((1,), (1,)), ((), ()))
    partial_value = lax.dot_general(
        gate_side, gate_full, across, preferred_element_type=jnp.float32
    )
    partial_value = partial_value + lax.dot_general(
        up_side, up_full, across, preferred_element_type=jnp.float32
    )
    rows_first = (((0,), (0,)), ((), ()))
    weight_terms = (
        lax.dot_general(slot_inputs, gate_side, rows_first, preferred_element_type=jnp.float32),
        lax.dot_general(slot_inputs, up_side, rows_first, preferred_element_type=jnp.float32),
        lax.dot_general(slot_grads, hidden, rows_first, preferred_element_type=jnp.float32),
    )
    return (partial_value.astype(jnp.bfloat16), weight_terms)


def body(
    layer_input, out_grad, routes, gate_values, keep_mask, gate_weight, up_weight, down_transposed
):
    devices = lax.axis_size("expert")
    live_count = devices // SPLIT
    token_count = layer_input.shape[0]
    model_width = layer_input.shape[1]
    weights = (
        lax.all_gather(gate_weight, "dp", axis=0, tiled=True),
        lax.all_gather(up_weight, "dp", axis=0, tiled=True),
        lax.all_gather(down_transposed, "dp", axis=0, tiled=True),
    )
    slot_count = MOST
    picked, filled = route_tables(routes, keep_mask, live_count, slot_count)
    token_of = picked // TOP
    route_scale = jnp.take(gate_values.reshape(-1), picked) * filled.astype(jnp.float32)
    sent_inputs = (
        jnp.take(layer_input, token_of, axis=0) * filled.astype(layer_input.dtype)[:, None]
    )
    sent_grads = (
        jnp.take(out_grad, token_of, axis=0).astype(jnp.float32) * route_scale[:, None]
    ).astype(jnp.bfloat16)
    expanded = (live_count, SPLIT, MOST, model_width)
    copies_in = jnp.broadcast_to(
        sent_inputs.reshape(live_count, 1, MOST, model_width), expanded
    ).reshape(-1, model_width)
    copies_grad = jnp.broadcast_to(
        sent_grads.reshape(live_count, 1, MOST, model_width), expanded
    ).reshape(-1, model_width)
    slot_inputs, slot_grads = (
        lax.all_to_all(copies_in, "expert", split_axis=0, concat_axis=0, tiled=True),
        lax.all_to_all(copies_grad, "expert", split_axis=0, concat_axis=0, tiled=True),
    )
    partial_value, weight_terms = expert_backward(slot_inputs, slot_grads, weights)
    returned = lax.all_to_all(partial_value, "expert", split_axis=0, concat_axis=0, tiled=True)
    summed = jnp.sum(
        returned.reshape(live_count, SPLIT, MOST, model_width).astype(jnp.float32), axis=1
    )
    summed = summed.reshape(-1, model_width)
    table_tokens = token_of.reshape(live_count, slot_count).reshape(-1)
    table_live = filled.reshape(live_count, slot_count).reshape(-1)
    token_iota = jnp.arange(token_count, dtype=jnp.int32)
    placing = ((token_iota[:, None] == table_tokens[None, :]) & (table_live[None, :] == 1)).astype(
        jnp.float32
    )
    input_grad = jnp.dot(
        placing, summed, precision=lax.Precision.HIGHEST, preferred_element_type=jnp.float32
    ).astype(jnp.bfloat16)
    rounded = tuple(
        (
            lax.optimization_barrier(weight_term.astype(jnp.bfloat16)).astype(jnp.float32)
            for weight_term in weight_terms
        )
    )
    gate_grad, up_grad, down_grad = jax.tree.map(
        lambda part: part.astype(jnp.float32),
        lax.psum_scatter(as_sent(rounded), "dp", scatter_dimension=0, tiled=True),
    )
    return (
        input_grad,
        gate_grad.astype(jnp.bfloat16),
        up_grad.astype(jnp.bfloat16),
        down_grad.astype(jnp.bfloat16),
    )


def solution(mesh):
    return jax.shard_map(
        body,
        mesh=mesh,
        in_specs=(
            P(("expert", "dp"), None),
            P(("expert", "dp"), None),
            P(("expert", "dp"), None),
            P(("expert", "dp"), None),
            P(("expert", "dp"), None),
            P("dp", "expert"),
            P("dp", "expert"),
            P("dp", "expert"),
        ),
        out_specs=(
            P(("expert", "dp"), None),
            P("dp", "expert"),
            P("dp", "expert"),
            P("dp", "expert"),
        ),
        check_vma=False,
    )
```

profile of v0, /device:TPU:2, one launch (start us, length us, event | category | flops | bytes accessed | tf_op | source)
XLA Modules:
  0.0 632.4 jit_solution(16840155601791492247)
XLA Ops:
  9.3 9.0 %reduce-window.6 = s32[32,8,128]{2,1,0:T(8,128)S(1)} reduce-window(s32[32,8,128]{2,1,0:T(8,128)S(1)} %fusion.6, s32[]{:T(128)} %constant.45.clone.1), window={size=1x1x128 pad=0_0x0_0x127_0}, to_apply=%region_0.0 | reduce-window | flops 4161536 | bytes 262148 | tf_op jit(solution)/shard_map/reduce-window
  24.4 1.5 broadcast_in_dim.38
  26.0 3.6 broadcast_in_dim.39
  29.6 16.0 %all-to-all-start = ((bf16[128,5,3584]{2,1,0:T(8,128)(2,1)}), bf16[128,5,3584]{2,1,0:T(8,128)(2,1)}, u32[]{:S(2)}, u32[]{:S(2)}) async-start(bf16[128,5,3584]{2,1,0:T(8,128)(2,1)} %bitcast.31), calls=%async_computation | async-start | bytes 14680064 | tf_op jit(solution)/shard_map/all_to_all | solution.py:94
  49.8 159.1 %all-to-all-done = bf16[128,5,3584]{2,1,0:T(8,128)(2,1)} async-done(((bf16[128,5,3584]{2,1,0:T(8,128)(2,1)}), bf16[128,5,3584]{2,1,0:T(8,128)(2,1)}, u32[]{:S(2)}, u32[]{:S(2)}) %all-to-all-start) | async-done | bytes 4587552 | tf_op jit(solution)/shard_map/all_to_all | solution.py:94
  208.9 3.5 broadcast_in_dim.41
  212.4 8.9 %all-to-all-start.1 = ((bf16[128,5,3584]{2,1,0:T(8,128)(2,1)}), bf16[128,5,3584]{2,1,0:T(8,128)(2,1)}, u32[]{:S(2)}, u32[]{:S(2)}) async-start(bf16[128,5,3584]{2,1,0:T(8,128)(2,1)} %bitcast.30), calls=%async_computation.1 | async-start | bytes 14680064 | tf_op jit(solution)/shard_map/all_to_all | solution.py:93
  223.7 8.1 %all_to_all.24 = bf16[640,3584]{1,0:T(8,128)(2,1)} reshape(bf16[128,5,3584]{2,1,0:T(8,128)(2,1)} %all-to-all-done) | data formatting | bytes 9175040 | tf_op jit(solution)/shard_map/all_to_all | solution.py:94
  231.8 152.7 %all-to-all-done.1 = bf16[128,5,3584]{2,1,0:T(8,128)(2,1)} async-done(((bf16[128,5,3584]{2,1,0:T(8,128)(2,1)}), bf16[128,5,3584]{2,1,0:T(8,128)(2,1)}, u32[]{:S(2)}, u32[]{:S(2)}) %all-to-all-start.1) | async-done | bytes 4587552 | tf_op jit(solution)/shard_map/all_to_all | solution.py:93
  384.5 8.1 %all_to_all.27 = bf16[640,3584]{1,0:T(8,128)(2,1)} reshape(bf16[128,5,3584]{2,1,0:T(8,128)(2,1)} %all-to-all-done.1) | data formatting | bytes 9175040 | tf_op jit(solution)/shard_map/all_to_all | solution.py:93
  392.6 5.7 fusion.15
  398.3 5.7 fusion.14
  405.0 6.7 %convolution_convert_fusion = bf16[3584,384]{1,0:T(8,128)(2,1)} fusion(bf16[640,3584]{1,0:T(8,128)(2,1)} %all_to_all.24, f32[640,384]{1,0:T(8,128)S(1)} %fusion.14, f32[640,384]{1,0:T(8,128)S(1)} %fusion.15), kind=kOutput, calls=%fused_computation.5 | convolution fusion | flops 1764458496 | bytes 9306112 | tf_op jit(solution)/shard_map/dot_general | solution.py:58
  412.0 6.1 multiply_convert_fusion.2
  418.1 7.5 %convolution_convert_fusion.1 = bf16[3584,384]{1,0:T(8,128)(2,1)} fusion(bf16[640,3584]{1,0:T(8,128)(2,1)} %all_to_all.27, bf16[640,384]{1,0:T(8,128)(2,1)S(1)} %get-tuple-element.9), kind=kOutput, calls=%fused_computation.6 | convolution fusion | flops 1762983936 | bytes 7831552 | tf_op jit(solution)/shard_map/dot_general | solution.py:57
  425.7 4.5 fusion.16
  430.2 4.7 add_convert_fusion
  434.9 8.2 %all_to_all.28 = bf16[128,5,3584]{2,1,0:T(8,128)(2,1)} reshape(bf16[640,3584]{1,0:T(8,128)(2,1)} %add_convert_fusion) | data formatting | bytes 9175040 | tf_op jit(solution)/shard_map/all_to_all | solution.py:97
  443.1 7.8 %all-to-all-start.2 = ((bf16[128,5,3584]{2,1,0:T(8,128)(2,1)}), bf16[128,5,3584]{2,1,0:T(8,128)(2,1)}, u32[]{:S(2)}, u32[]{:S(2)}) async-start(bf16[128,5,3584]{2,1,0:T(8,128)(2,1)} %all_to_all.28), calls=%async_computation.2 | async-start | bytes 14680064 | tf_op jit(solution)/shard_map/all_to_all | solution.py:97
  451.2 6.8 %convolution_convert_fusion.2 = bf16[3584,384]{1,0:T(8,128)(2,1)} fusion(bf16[640,3584]{1,0:T(8,128)(2,1)} %all_to_all.27, bf16[640,384]{1,0:T(8,128)(2,1)S(1)} %get-tuple-element.10), kind=kOutput, calls=%fused_computation.7 | convolution fusion | flops 1762983936 | bytes 7831552 | tf_op jit(solution)/shard_map/dot_general | solution.py:56
  458.3 155.8 %all-to-all-done.2 = bf16[128,5,3584]{2,1,0:T(8,128)(2,1)} async-done(((bf16[128,5,3584]{2,1,0:T(8,128)(2,1)}), bf16[128,5,3584]{2,1,0:T(8,128)(2,1)}, u32[]{:S(2)}, u32[]{:S(2)}) %all-to-all-start.2) | async-done | bytes 4587552 | tf_op jit(solution)/shard_map/all_to_all | solution.py:97
  614.1 6.9 %convert_reduce_fusion = f32[32,5,3584]{2,1,0:T(8,128)} fusion(bf16[128,5,3584]{2,1,0:T(8,128)(2,1)} %all-to-all-done.2), kind=kLoop, calls=%fused_computation.3 | loop fusion | flops 4014080 | bytes 6881280 | tf_op jit(solution)/shard_map/reduce_sum | solution.py:98
  621.1 2.4 reshape.220
  623.4 2.1 convolution_convert_fusion.3
  (70 shorter events, 16.6 us)
Async XLA Ops:
  7.2 14.6 %copy-start = (bf16[128,3584]{1,0:T(8,128)(2,1)S(1)}, bf16[128,3584]{1,0:T(8,128)(2,1)}, u32[]{:S(2)}) copy-start(bf16[128,3584]{1,0:T(8,128)(2,1)} %param.11) | copy-start | bytes 2752516
  29.6 16.2 %copy-start.2 = (bf16[128,3584]{1,0:T(8,128)(2,1)S(1)}, bf16[128,3584]{1,0:T(8,128)(2,1)}, u32[]{:S(2)}) copy-start(bf16[128,3584]{1,0:T(8,128)(2,1)} %param.10) | copy-start | bytes 2752516
  29.6 179.3 %all-to-all-start = ((bf16[128,5,3584]{2,1,0:T(8,128)(2,1)}), bf16[128,5,3584]{2,1,0:T(8,128)(2,1)}, u32[]{:S(2)}, u32[]{:S(2)}) async-start(bf16[128,5,3584]{2,1,0:T(8,128)(2,1)} %bitcast.31), calls=%async_computation | async-start | bytes 14680064 | tf_op jit(solution)/shard_map/all_to_all | solution.py:94
  212.4 172.1 %all-to-all-start.1 = ((bf16[128,5,3584]{2,1,0:T(8,128)(2,1)}), bf16[128,5,3584]{2,1,0:T(8,128)(2,1)}, u32[]{:S(2)}, u32[]{:S(2)}) async-start(bf16[128,5,3584]{2,1,0:T(8,128)(2,1)} %bitcast.30), calls=%async_computation.1 | async-start | bytes 14680064 | tf_op jit(solution)/shard_map/all_to_all | solution.py:93
  221.3 171.3 %all-gather.8.cloned.1.call-start = ((), (), s32[]{:S(2)}) async-start(), calls=%async_computation.8 | async-start | bytes 4128768 | tf_op jit(solution)/shard_map/all_gather | solution.py:71
  222.0 176.3 %all-gather.6.cloned.1.call-start = ((), (), s32[]{:S(2)}) async-start(), calls=%async_computation.7 | async-start | bytes 4128768 | tf_op jit(solution)/shard_map/all_gather | solution.py:72
  222.8 189.2 %all-gather.4.cloned.1.call-start = ((), (), s32[]{:S(2)}) async-start(), calls=%async_computation.6 | async-start | bytes 4128768 | tf_op jit(solution)/shard_map/all_gather | solution.py:73
  223.5 402.1 %reduce-scatter.8.cloned.1.call-start = ((), (), s32[]{:S(2)}) async-start(), calls=%async_computation.11 | async-start | bytes 4128768 | tf_op jit(solution)/shard_map/reduce_scatter | solution.py:119
  404.0 0.9 copy-start.4
  411.7 213.9 %reduce-scatter.6.cloned.1.call-start = ((), (), s32[]{:S(2)}) async-start(), calls=%async_computation.10 | async-start | bytes 4128768 | tf_op jit(solution)/shard_map/reduce_scatter | solution.py:119
  425.7 4.5 copy-start.3
  443.1 171.0 %all-to-all-start.2 = ((bf16[128,5,3584]{2,1,0:T(8,128)(2,1)}), bf16[128,5,3584]{2,1,0:T(8,128)(2,1)}, u32[]{:S(2)}, u32[]{:S(2)}) async-start(bf16[128,5,3584]{2,1,0:T(8,128)(2,1)} %all_to_all.28), calls=%async_computation.2 | async-start | bytes 14680064 | tf_op jit(solution)/shard_map/all_to_all | solution.py:97
  450.9 174.7 %reduce-scatter.4.cloned.1.call-start = ((), (), s32[]{:S(2)}) async-start(), calls=%async_computation.9 | async-start | bytes 4128768 | tf_op jit(solution)/shard_map/reduce_scatter | solution.py:119
  621.1 4.5 copy-start.1
Sparse Core Ops, SparseCore 0:
  223.9 18.1 all-gather.7
  243.9 18.1 all-gather.5
  263.9 18.1 all-gather.3
  411.8 11.6 reduce-scatter.7
  426.6 16.9 reduce-scatter.5
  458.2 16.9 reduce-scatter.3
where the time goes:
time: 634 us; the launch traced here: 632 us
  waiting for transfers between devices  470 us (74%)
  matrix products  49.9 us (8%)
  local copies, waits for them, and re-layouts  44.9 us (7%)
  starting transfers between devices  33.6 us (5%)
  other arithmetic  19.8 us (3%)
  between operations  14.4 us (2%)
    all_to_all x1, waiting for transfers between devices, body(): lax.all_to_all(copies_grad, 'expert', split_axis=0, concat_axis=0, tiled=...  159 us
    all_to_all x1, waiting for transfers between devices, body(): lax.all_to_all(partial_value, 'expert', split_axis=0, concat_axis=0, tile...  156 us
    all_to_all x1, waiting for transfers between devices, body(): lax.all_to_all(copies_in, 'expert', split_axis=0, concat_axis=0, tiled=True)  153 us
    all_to_all x1, starting transfers between devices, body(): lax.all_to_all(copies_grad, 'expert', split_axis=0, concat_axis=0, tiled=...  16 us
  transfers between devices with their start and end apart: 9, of which 3 were waited for; matrix products, arithmetic and copies ran while one was open for 10% of the time, Pallas kernels for 0%

commit v1 on v0

v1 whole, which is shorter than its diff:
```python
import functools

import jax
import jax.numpy as jnp
from jax import lax
from jax.experimental import pallas as pl
from jax.experimental.pallas import tpu as pltpu
from jax.sharding import PartitionSpec as P

NX, NY, NZ = 4, 4, 8
NP = NY * NZ
MOST = 5
QUART = 896
MESH = pl.DeviceIdType.MESH
VMEM_CAP = 64 * 1024 * 1024 - 512 * 1024
F32 = jnp.float32
BF16 = jnp.bfloat16


def vmem():
    return pl.BlockSpec(memory_space=pltpu.VMEM)


def hbm():
    return pl.BlockSpec(memory_space=pl.ANY)


def params(**kw):
    return pltpu.CompilerParams(vmem_limit_bytes=VMEM_CAP, **kw)


def iota(shape, dim):
    return lax.broadcasted_iota(jnp.int32, shape, dim)


def by_five(v):
    return (v * 205) >> 10


def as_bf16(flag):
    return jnp.where(flag, 1.0, 0.0).astype(BF16)


def pack_kernel(routes_ref, keep_ref, gate_ref, in_ref, grad_ref, send_ref, pick_ref):
    rows, tok = pick_ref.shape
    width = in_ref.shape[1]
    row = iota((rows, tok), 0)
    expert, place = row >> 3, row & 7
    live = jnp.zeros((rows, tok), F32)
    scale = jnp.zeros((rows, tok), F32)
    for k in range(routes_ref.shape[0]):
        hit = (routes_ref[k : k + 1, :] == expert) & (keep_ref[k : k + 1, :] == 1)
        live = jnp.where(hit, 1.0, live)
        scale = jnp.where(hit, gate_ref[k : k + 1, :], scale)
    before = as_bf16(iota((tok, tok), 0) < iota((tok, tok), 1))
    rank = jnp.dot(live.astype(BF16), before, preferred_element_type=F32).astype(jnp.int32)
    alive = live > 0.5
    is_input = place < MOST
    pick_ref[...] = as_bf16(alive & is_input & (rank == place))
    main = alive & (rank == jnp.where(is_input, place, place - MOST))
    tail = alive & (rank == 3 + (place >> 2))
    main_scale = jnp.sum(jnp.where(main, scale, 0.0), axis=1, keepdims=True)
    main_scale = jnp.where(is_input[:, :1], 1.0, main_scale)
    tail_scale = jnp.sum(jnp.where(tail, scale, 0.0), axis=1, keepdims=True)
    from_input = as_bf16(main & is_input)
    from_grad = as_bf16(main & jnp.logical_not(is_input))
    total = jnp.zeros((rows, QUART), F32)
    for p in range(width // QUART):
        cols = slice(p * QUART, (p + 1) * QUART)
        got = jnp.dot(from_input, in_ref[:, cols], preferred_element_type=F32)
        got = got + jnp.dot(from_grad, grad_ref[:, cols], preferred_element_type=F32)
        send_ref[:, cols] = (got * main_scale).astype(BF16)
        piece = as_bf16(tail & ((place & 3) == p))
        total = total + jnp.dot(piece, grad_ref[:, cols], preferred_element_type=F32)
    send_ref[:, width:] = (total * tail_scale).astype(BF16)


def place_of():
    me = lax.axis_index("expert")
    x, p = lax.rem(me, NX), lax.div(me, NX)
    return x, lax.rem(p, NY), lax.div(p, NY), p


def offset_of(j):
    k = lax.div(j, NY)
    dz = lax.div(k + 1, 2) * (2 * lax.rem(k, 2) - 1)
    return lax.rem(j, NY), dz


def plane_index(y, z, dy, dz):
    return lax.rem(z + dz + NZ, NZ) * NY + lax.rem(y + dy + NY, NY)


def greet(x, y, z, p):
    dp = lax.axis_index("dp")
    barrier = pltpu.get_barrier_semaphore()
    right = (p * NX + lax.rem(x + 1, NX), dp)
    left = (p * NX + lax.rem(x + NX - 1, NX), dp)
    for other in (left, right):
        pl.semaphore_signal(barrier, inc=1, device_id=other, device_id_type=MESH)

    def one(j, carry):
        dy, dz = offset_of(j)
        q = plane_index(y, z, dy, dz)
        pl.semaphore_signal(barrier, inc=1, device_id=(q * NX + x, dp), device_id_type=MESH)
        return carry

    lax.fori_loop(1, NP, one, 0)
    pl.semaphore_wait(barrier, NP + 1)
    return left, right, dp


LAG = 4


def dispatch_kernel(
    send_ref, out_ref, own_sem, plane_send, plane_recv, ring_send, left_recv, right_recv, far_recv
):
    x, y, z, p = place_of()
    left, right, dp = greet(x, y, z, p)

    def ring_copy(src, block, j, recv, device):
        return pltpu.make_async_remote_copy(
            src_ref=src,
            dst_ref=out_ref.at[block, j],
            send_sem=ring_send,
            recv_sem=recv.at[j],
            device_id=device,
            device_id_type=MESH,
        )

    own = pltpu.make_async_copy(send_ref.at[p], out_ref.at[0, 0], own_sem)
    own.start()

    def plane_copy(j):
        dy, dz = offset_of(j)
        q = plane_index(y, z, dy, dz)
        return pltpu.make_async_remote_copy(
            src_ref=send_ref.at[q],
            dst_ref=out_ref.at[0, j],
            send_sem=plane_send,
            recv_sem=plane_recv.at[j],
            device_id=(q * NX + x, dp),
            device_id_type=MESH,
        )

    def start_plane(j, carry):
        plane_copy(j).start()
        return carry

    ring_copy(send_ref.at[p], 1, 0, left_recv, right).start()
    ring_copy(send_ref.at[p], 2, 0, right_recv, left).start()
    lax.fori_loop(1, NP, start_plane, 0)

    def relay_far(j):
        @pl.when(lax.rem(j, 2) == 0)
        def _():
            ring_copy(out_ref.at[1, j], 1, j, left_recv, right).wait_recv()
            ring_copy(out_ref.at[1, j], 3, j, far_recv, right).start()

        @pl.when(lax.rem(j, 2) == 1)
        def _():
            ring_copy(out_ref.at[2, j], 2, j, right_recv, left).wait_recv()
            ring_copy(out_ref.at[2, j], 3, j, far_recv, left).start()

    def step(j, carry):
        plane_copy(j).wait_recv()
        ring_copy(out_ref.at[0, j], 1, j, left_recv, right).start()
        ring_copy(out_ref.at[0, j], 2, j, right_recv, left).start()

        @pl.when(j >= LAG)
        def _():
            relay_far(j - LAG)

        return carry

    lax.fori_loop(1, NP, step, 0)

    def drain(j, carry):
        relay_far(j)
        return carry

    lax.fori_loop(NP - LAG, NP, drain, 0)

    def rest(j, carry):
        @pl.when(lax.rem(j, 2) == 1)
        def _():
            ring_copy(out_ref.at[1, j], 1, j, left_recv, right).wait_recv()

        @pl.when(lax.rem(j, 2) == 0)
        def _():
            ring_copy(out_ref.at[2, j], 2, j, right_recv, left).wait_recv()

        ring_copy(out_ref.at[0, j], 3, j, far_recv, right).wait_recv()
        return carry

    lax.fori_loop(0, NP, rest, 0)
    own.wait()
    pltpu.make_async_copy(
        out_ref.at[0, pl.ds(0, NP - 1)], out_ref.at[0, pl.ds(0, NP - 1)], plane_send
    ).wait()
    pltpu.make_async_copy(
        out_ref.at[pl.ds(0, 3)], out_ref.at[pl.ds(0, 3)], ring_send
    ).wait()


def expert_kernel(
    got_ref, gate_w, up_w, down_w, part_ref, gate_out, up_out, down_out,
    got, both_w, down_v, xs, ss, pre, hgrad, sides, hidden, got_sem, w_sem,
):
    group = NP * MOST
    span = NP * 8
    width = xs.shape[1]
    hid = down_v.shape[1]
    loads = [
        pltpu.make_async_copy(got_ref.at[b], got.at[b], got_sem.at[b]) for b in range(NX)
    ]
    for load in loads:
        load.start()
    w_loads = [
        pltpu.make_async_copy(gate_w, both_w.at[:, pl.ds(0, hid)], w_sem.at[0]),
        pltpu.make_async_copy(up_w, both_w.at[:, pl.ds(hid, hid)], w_sem.at[1]),
        pltpu.make_async_copy(down_w, down_v, w_sem.at[2]),
    ]
    for load in w_loads:
        load.start()

    slot, place = iota((group, span), 0), iota((group, span), 1)
    which = slot - MOST * by_five(slot)
    same = (place >> 3) == by_five(slot)
    inner = place & 7
    take_x = as_bf16(same & (inner == which))
    take_s = as_bf16(same & (inner == which + MOST))
    take_t = [
        as_bf16(same & (which >= 3) & (inner == (which - 3) * 4 + p)) for p in range(width // QUART)
    ]
    for b in range(NX):
        loads[b].wait()
        rows = slice(b * group, (b + 1) * group)
        rest = got[b, :, width:]
        for p in range(width // QUART):
            cols = slice(p * QUART, (p + 1) * QUART)
            block = got[b, :, cols]
            xs[rows, cols] = jnp.dot(take_x, block, preferred_element_type=F32).astype(BF16)
            picked = jnp.dot(take_s, block, preferred_element_type=F32)
            picked = picked + jnp.dot(take_t[p], rest, preferred_element_type=F32)
            ss[rows, cols] = picked.astype(BF16)

    w_loads[0].wait()
    w_loads[1].wait()

    @pl.loop(0, 2 * hid // 256)
    def _(n):
        cols = pl.ds(pl.multiple_of(n * 256, 256), 256)
        pre[:, cols] = jnp.dot(xs[...], both_w[:, cols], preferred_element_type=F32)

    w_loads[2].wait()
    hgrad[...] = jnp.dot(ss[...], down_v[...], preferred_element_type=F32)

    @pl.loop(0, NX * group // 64)
    def _(i):
        rows = pl.ds(pl.multiple_of(i * 64, 64), 64)
        gate, up, hg = pre[rows, :hid], pre[rows, hid:], hgrad[rows, :]
        sigma = jax.nn.sigmoid(gate)
        activated = gate * sigma
        hidden[rows, :] = (activated * up).astype(BF16)
        slope = sigma * (1.0 + gate * (1.0 - sigma))
        sides[rows, :hid] = (hg * up * slope).astype(BF16)
        sides[rows, hid:] = (hg * activated).astype(BF16)

    across = (((1,), (1,)), ((), ()))
    down = (((0,), (0,)), ((), ()))

    @pl.loop(0, width // 512)
    def _(n):
        cols = pl.ds(pl.multiple_of(n * 512, 512), 512)
        part_ref[:, cols] = lax.dot_general(
            sides[...], both_w[cols, :], across, preferred_element_type=F32
        ).astype(BF16)

    @pl.loop(0, width // 512)
    def _(n):
        cols = pl.ds(pl.multiple_of(n * 512, 512), 512)
        term = lax.dot_general(xs[:, cols], sides[...], down, preferred_element_type=F32)
        gate_out[cols, :] = term[:, :hid].astype(BF16)
        up_out[cols, :] = term[:, hid:].astype(BF16)
        term = lax.dot_general(ss[:, cols], hidden[...], down, preferred_element_type=F32)
        down_out[cols, :] = term.astype(BF16)


CH = 8
ROWS = CH * MOST
NC = NP // CH


def return_kernel(
    part_ref, ret_ref, half, pass_on, near_left, near_right, message,
    far_recv, left_recv, right_recv, ring_send, plane_send, plane_recv, own_sem,
):
    x, y, z, p = place_of()
    left, right, dp = greet(x, y, z, p)

    def ring_copy(src, dst, recv, device):
        return pltpu.make_async_remote_copy(
            src_ref=src, dst_ref=dst, send_sem=ring_send, recv_sem=recv,
            device_id=device, device_id_type=MESH,
        )

    def rows_of(block, k):
        return part_ref.at[pl.ds((block * NC + k) * ROWS, ROWS)]

    def far(k):
        return ring_copy(rows_of(3, k), half.at[k], far_recv.at[k], right if k % 2 == 0 else left)

    def direct(k):
        if k % 2 == 0:
            return ring_copy(rows_of(1, k), near_right.at[k], right_recv.at[k], left)
        return ring_copy(rows_of(2, k), near_left.at[k], left_recv.at[k], right)

    def summed(k):
        if k % 2 == 0:
            return ring_copy(pass_on.at[k], near_left.at[k], left_recv.at[k], right)
        return ring_copy(pass_on.at[k], near_right.at[k], right_recv.at[k], left)

    def plane_copy(j):
        dy, dz = offset_of(j)
        q = plane_index(y, z, -dy, -dz)
        return pltpu.make_async_remote_copy(
            src_ref=message.at[j], dst_ref=ret_ref.at[p], send_sem=plane_send, recv_sem=plane_recv,
            device_id=(q * NX + x, dp), device_id_type=MESH,
        )

    far(0).start()
    far(1).start()
    direct(0).start()
    direct(1).start()
    far(2).start()
    far(3).start()
    direct(2).start()
    direct(3).start()
    for k in range(NC):
        far(k).wait_recv()
        block = 2 if k % 2 == 0 else 1
        mine = part_ref[pl.ds((block * NC + k) * ROWS, ROWS), :].astype(F32)
        pass_on[k] = (mine + half[k].astype(F32)).astype(BF16)
        summed(k).start()
    spread_row, spread_col = iota((CH * 8, ROWS), 0), iota((CH * 8, ROWS), 1)
    spread = as_bf16(
        ((spread_row >> 3) == by_five(spread_col))
        & ((spread_row & 7) == spread_col - MOST * by_five(spread_col))
    )
    for k in range(NC):
        ring_copy(pass_on.at[k], near_left.at[k], left_recv.at[k], right).wait_recv()
        ring_copy(pass_on.at[k], near_right.at[k], right_recv.at[k], left).wait_recv()
        total = part_ref[pl.ds(k * ROWS, ROWS), :].astype(F32)
        total = total + near_left[k].astype(F32) + near_right[k].astype(F32)
        out = jnp.dot(spread, total.astype(BF16), preferred_element_type=F32).astype(BF16)
        message[pl.ds(k * CH, CH)] = out.reshape(CH, 8, out.shape[1])

        def start_plane(j, carry):
            plane_copy(j).start()
            return carry

        lax.fori_loop(max(1, k * CH), (k + 1) * CH, start_plane, 0)
        if k == 0:
            own = pltpu.make_async_copy(message.at[0], ret_ref.at[p], own_sem)
            own.start()
    own.wait()
    most = pl.ds(0, NP - 1)
    pltpu.make_async_copy(message.at[most], message.at[most], plane_recv).wait()
    pltpu.make_async_copy(message.at[most], message.at[most], plane_send).wait()
    pltpu.make_async_copy(
        part_ref.at[pl.ds(0, 3 * NC * ROWS)], part_ref.at[pl.ds(0, 3 * NC * ROWS)], ring_send
    ).wait()


def combine_kernel(pick_ref, ret_ref, out_ref):
    width = out_ref.shape[1]

    @pl.loop(0, width // 512)
    def _(n):
        cols = pl.ds(pl.multiple_of(n * 512, 512), 512)
        out_ref[:, cols] = lax.dot_general(
            pick_ref[...], ret_ref[:, cols], (((0,), (0,)), ((), ())), preferred_element_type=F32
        ).astype(BF16)


def body(layer_input, out_grad, routes, gate_values, keep_mask, gate_weight, up_weight, down_w):
    tok, width = layer_input.shape
    hid = gate_weight.shape[1]
    group = NP * MOST
    span = NP * 8
    packed = width + QUART
    dma = pltpu.SemaphoreType.DMA

    def shape(*dims, dtype=BF16):
        return jax.ShapeDtypeStruct(dims, dtype)

    weights = [
        lax.all_gather(w, "dp", axis=0, tiled=True) for w in (gate_weight, up_weight, down_w)
    ]
    send, pick = pl.pallas_call(
        pack_kernel,
        out_shape=(shape(span, packed), shape(span, tok)),
        in_specs=[vmem()] * 5,
        out_specs=(vmem(), vmem()),
        compiler_params=params(),
        name="pack",
    )(routes.T, keep_mask.T, gate_values.T, layer_input, out_grad)
    got = pl.pallas_call(
        dispatch_kernel,
        out_shape=shape(NX, NP, 8, packed),
        in_specs=[hbm()],
        out_specs=hbm(),
        scratch_shapes=[dma, dma, dma((NP,)), dma, dma((NP,)), dma((NP,)), dma((NP,))],
        compiler_params=params(collective_id=0, has_side_effects=True),
        cost_estimate=pl.CostEstimate(flops=0, bytes_accessed=300_000_000, transcendentals=0),
        name="dispatch",
    )(send.reshape(NP, 8, packed))
    parts, gate_term, up_term, down_term = pl.pallas_call(
        expert_kernel,
        out_shape=(
            shape(NX * group, width),
            shape(width, hid),
            shape(width, hid),
            shape(width, hid),
        ),
        in_specs=[hbm()] * 4,
        out_specs=(vmem(),) * 4,
        scratch_shapes=[
            pltpu.VMEM((NX, span, packed), BF16),
            pltpu.VMEM((width, 2 * hid), BF16),
            pltpu.VMEM((width, hid), BF16),
            pltpu.VMEM((NX * group, width), BF16),
            pltpu.VMEM((NX * group, width), BF16),
            pltpu.VMEM((NX * group, 2 * hid), F32),
            pltpu.VMEM((NX * group, hid), F32),
            pltpu.VMEM((NX * group, 2 * hid), BF16),
            pltpu.VMEM((NX * group, hid), BF16),
            dma((NX,)),
            dma((3,)),
        ],
        compiler_params=params(),
        name="expert",
    )(got.reshape(NX, span, packed), *weights)
    ret = pl.pallas_call(
        return_kernel,
        out_shape=shape(NP, 8, width),
        in_specs=[vmem()],
        out_specs=vmem(),
        scratch_shapes=[
            pltpu.VMEM((NC, ROWS, width), BF16),
            pltpu.VMEM((NC, ROWS, width), BF16),
            pltpu.VMEM((NC, ROWS, width), BF16),
            pltpu.VMEM((NC, ROWS, width), BF16),
            pltpu.VMEM((NP, 8, width), BF16),
            dma((NC,)),
            dma((NC,)),
            dma((NC,)),
            dma,
            dma,
            dma,
            dma,
        ],
        compiler_params=params(collective_id=1, has_side_effects=True),
        cost_estimate=pl.CostEstimate(flops=0, bytes_accessed=200_000_000, transcendentals=0),
        name="return",
    )(parts)
    input_grad = pl.pallas_call(
        combine_kernel,
        out_shape=shape(tok, width),
        in_specs=[vmem()] * 2,
        out_specs=vmem(),
        compiler_params=params(),
        name="combine",
    )(pick, ret.reshape(span, width))
    gate_grad, up_grad, down_grad = [
        lax.psum_scatter(term, "dp", scatter_dimension=0, tiled=True)
        for term in (gate_term, up_term, down_term)
    ]
    return input_grad, gate_grad, up_grad, down_grad


def solution(mesh):
    rows = P(("expert", "dp"), None)
    cols = P("dp", "expert")
    return jax.shard_map(
        body,
        mesh=mesh,
        in_specs=(rows,) * 5 + (cols,) * 3,
        out_specs=(rows, cols, cols, cols),
        check_vma=False,
    )
```

time: 634 us -> 239 us (0.38)
  waiting for transfers between devices: 470 us -> 3.19 us
  Pallas kernels: 0 us -> 221 us
  matrix products: 49.9 us -> 0 us
  local copies, waits for them, and re-layouts: 44.9 us -> 0 us
  starting transfers between devices: 33.6 us -> 0.23 us
  other arithmetic: 19.8 us -> 0 us
    all_to_all x3 -> x0, waiting for transfers between devices: 468 us -> none  [the longest x1 159 us: body(): lax.all_to_all(copies_grad, 'expert', split_axis=0, concat_axis=0, tiled=...]
    pallas_call x0 -> x5, Pallas kernels: none -> 221 us  [the longest x1 99.2 us: body(): pl.pallas_call(dispatch_kernel, out_shape=shape(NX, NP, 8, packed), in_sp...]
    dot_general x9 -> x0, matrix products: 49.9 us -> none  [the longest x1 7.54 us: expert_backward(): lax.dot_general(slot_inputs, up_side, rows_first, preferred_element_type=...]
    all_to_all x3 -> x0, starting transfers between devices: 32.7 us -> none  [the longest x1 16 us: body(): lax.all_to_all(copies_grad, 'expert', split_axis=0, concat_axis=0, tiled=...]
    all_to_all x3 -> x0, local copies, waits for them, and re-layouts: 24.3 us -> none  [the longest x1 8.15 us: body(): lax.all_to_all(partial_value, 'expert', split_axis=0, concat_axis=0, tile...]
    broadcast_in_dim x4 -> x0, local copies, waits for them, and re-layouts: 10.1 us -> none  [the longest x2 5.11 us: body(): jnp.broadcast_to(sent_grads.reshape(live_count, 1, MOST, model_width), ex...]
    another operation x2 -> x0, other arithmetic: 9.04 us -> none
    reduce_sum x2 -> x0, other arithmetic: 7.24 us -> none  [the longest x1 6.95 us: body(): jnp.sum(returned.reshape(live_count, SPLIT, MOST, model_width).astype(jnp...]
  transfers between devices with their start and end apart: 9 -> 6, of which waited for: 3 -> 0; matrix products, arithmetic and copies ran while one was open for 10% -> 0% of each run, Pallas kernels for 0% -> 80%
where the time goes in v1:
time: 239 us
  Pallas kernels  221 us (92%)
  between operations  14.2 us (6%)
  waiting for transfers between devices  3.19 us (1%)
    pallas_call x1, Pallas kernels, body(): pl.pallas_call(dispatch_kernel, out_shape=shape(NX, NP, 8, packed), in_sp...  99.2 us
    pallas_call x1, Pallas kernels, body(): pl.pallas_call(return_kernel, out_shape=shape(NP, 8, width), in_specs=[vm...  82.8 us
    pallas_call x1, Pallas kernels, body(): pl.pallas_call(expert_kernel, out_shape=(shape(NX * group, width), shape(...  30.5 us
  transfers between devices with their start and end apart: 6, of which 0 were waited for; matrix products, arithmetic and copies ran while one was open for 0% of the time, Pallas kernels for 80%

profile of v1, /device:TPU:2, one launch (start us, length us, event | category | flops | bytes accessed | tf_op | source)
XLA Modules:
  0.0 238.7 jit_solution(6500143201264773788)
XLA Ops:
  7.2 0.0 all-gather.4.cloned.1.call-start
  7.2 0.7 all-gather.4.cloned.1.call-update
  7.9 0.0 all-gather.6.cloned.1.call-start
  7.9 0.7 all-gather.6.cloned.1.call-update
  8.6 0.0 all-gather.8.cloned.1.call-start
  8.7 0.7 all-gather.8.cloned.1.call-update
  9.4 0.0 reduce-scatter.4.cloned.1.call-start
  9.4 4.8 %pack.1 = (bf16[256,4480]{1,0:T(8,128)(2,1)}, bf16[256,128]{1,0:T(8,128)(2,1)}) custom-call(s32[8,128]{1,0:T(8,128)} %bitcast.9, s32[8,128]{1,0:T(8,128)} %bitcast.10, f32[8,128]{1,0:T(8,128)} %bitcast.11, bf16[128,3584]{1,0:T(8,128)(2,1)} %in_ref.1, bf16[128,3584]{1,0:T(8,128)(2,1)} %grad_ref.1), custom_call_target="tpu_custom_call" | custom-call | tf_op jit(solution)/shard_map/pack/pallas_call | solution.py:402
  14.2 99.2 %dispatch.1 = bf16[4,32,8,4480]{3,2,1,0:T(8,128)(2,1)} custom-call(bf16[32,8,4480]{2,1,0:T(8,128)(2,1)} %bitcast.8), custom_call_target="tpu_custom_call" | custom-call | bytes 300000000 | tf_op jit(solution)/shard_map/dispatch/pallas_call | solution.py:410
  113.4 0.0 all-gather.4.cloned.1.call-done.gate_w
  113.4 0.0 all-gather.6.cloned.1.call-done.up_w
  113.4 0.0 all-gather.8.cloned.1.call-done.down_w
  113.4 30.5 %expert.1 = (bf16[640,3584]{1,0:T(8,128)(2,1)}, bf16[3584,384]{1,0:T(8,128)(2,1)}, bf16[3584,384]{1,0:T(8,128)(2,1)}, bf16[3584,384]{1,0:T(8,128)(2,1)}) custom-call(bf16[4,256,4480]{2,1,0:T(8,128)(2,1)} %bitcast.6, bf16[3584,384]{1,0:T(8,128)(2,1)} %all-gather.4.cloned.1.call-done.gate_w, bf16[3584,384]{1,0:T(8,128)(2,1)} %all-gather.6.cloned.1.call-done.up_w, ...), custom_call_target="tpu_custom_call" | custom-call | tf_op jit(solution)/shard_map/expert/pallas_call | solution.py:420
  143.9 0.0 reduce-scatter.4.cloned.1.call-update
  144.0 0.0 reduce-scatter.6.cloned.1.call-start
  144.0 0.5 reduce-scatter.6.cloned.1.call-update
  144.5 0.0 reduce-scatter.8.cloned.1.call-start
  144.6 0.5 reduce-scatter.8.cloned.1.call-update
  145.1 82.8 %return.1 = bf16[32,8,3584]{2,1,0:T(8,128)(2,1)} custom-call(bf16[640,3584]{1,0:T(8,128)(2,1)} %get-tuple-element.12.part_ref), custom_call_target="tpu_custom_call" | custom-call | bytes 200000000 | tf_op jit(solution)/shard_map/return/pallas_call | solution.py:446
  227.9 3.9 %combine.1 = bf16[128,3584]{1,0:T(8,128)(2,1)} custom-call(bf16[256,128]{1,0:T(8,128)(2,1)} %get-tuple-element.10.pick_ref, bf16[256,3584]{1,0:T(8,128)(2,1)} %bitcast.7), custom_call_target="tpu_custom_call" | custom-call | tf_op jit(solution)/shard_map/combine/pallas_call | solution.py:469
  231.8 0.0 reduce-scatter.4.cloned.1.call-done
  231.8 0.0 reduce-scatter.6.cloned.1.call-done
  231.8 0.0 reduce-scatter.8.cloned.1.call-done
Async XLA Ops:
  7.2 106.2 %all-gather.4.cloned.1.call-start = ((), (), s32[]{:S(2)}) async-start(), calls=%async_computation.3 | async-start | bytes 4128768 | tf_op jit(solution)/shard_map/all_gather | solution.py:400
  7.9 105.5 %all-gather.6.cloned.1.call-start = ((), (), s32[]{:S(2)}) async-start(), calls=%async_computation.4 | async-start | bytes 4128768 | tf_op jit(solution)/shard_map/all_gather | solution.py:400
  8.6 104.8 %all-gather.8.cloned.1.call-start = ((), (), s32[]{:S(2)}) async-start(), calls=%async_computation.5 | async-start | bytes 4128768 | tf_op jit(solution)/shard_map/all_gather | solution.py:400
  9.4 222.5 %reduce-scatter.4.cloned.1.call-start = ((), (), s32[]{:S(2)}) async-start(), calls=%async_computation.6 | async-start | bytes 4128768 | tf_op jit(solution)/shard_map/reduce_scatter | solution.py:478
  144.0 87.9 %reduce-scatter.6.cloned.1.call-start = ((), (), s32[]{:S(2)}) async-start(), calls=%async_computation.7 | async-start | bytes 4128768 | tf_op jit(solution)/shard_map/reduce_scatter | solution.py:478
  144.5 87.3 %reduce-scatter.8.cloned.1.call-start = ((), (), s32[]{:S(2)}) async-start(), calls=%async_computation.8 | async-start | bytes 4128768 | tf_op jit(solution)/shard_map/reduce_scatter | solution.py:478
Sparse Core Ops, SparseCore 0:
  9.8 19.8 all-gather.3
  31.4 18.1 all-gather.5
  51.5 18.1 all-gather.7
  144.1 11.0 reduce-scatter.3
  158.3 16.9 reduce-scatter.5
  178.2 17.0 reduce-scatter.7
